TPU v7x, 256 devices: a whole 4x4x8 slice. The times are simulated.
256 devices in a mesh: feat: 32 (over y, z), dp: 8 (over x, core).
Axes of the slice: x: 4, y: 4, z: 8, core: 2. Of those that a mesh axis runs over, the one named last changes fastest.
Arguments:
- face_grid: bfloat16 [32768, 10240], P('dp', 'feat'), may hold values from -6 to 6
- first_nbrs: int32 [16384, 8], P('dp'), may hold values from 0 to 4095
- first_count: int32 [16384], P('dp'), may hold values from 1 to 8
- w_first: bfloat16 [10240, 256], P('feat'), may hold values from -0.0625 to 0.0625
- b_first: float32 [256], replicated, may hold values from -3 to 3
- send_rows: int32 [4096], P('dp'), may hold values from 0 to 2047
- second_nbrs: int32 [16384, 8], P(('dp', 'feat')), may hold values from 0 to 2559
- second_count: int32 [16384], P(('dp', 'feat')), may hold values from 1 to 8
- w_in: bfloat16 [256, 1024], replicated, may hold values from -0.375 to 0.375
- w_out: bfloat16 [1024, 256], replicated, may hold values from -0.1875 to 0.1875
- out_grad: bfloat16 [16384, 256], P(('dp', 'feat')), may hold values from -6 to 6
Outputs:
- embed: bfloat16 [16384, 256], P(('dp', 'feat'))
- grad_first: float32 [10240, 256], P('feat')
Inputs may be any that keep to these rules, and one draw needn't show every extreme that they name: `first_count`: slots at or past a target's count are ignored; counts lie in 1 to 8. `first_nbrs`: only slots below first_count are read. `second_count`: slots at or past a target's count are ignored. `second_nbrs`: indices below 2048 name the partition's own targets, the rest the faces received from the previous partition in order; only slots below second_count are read. `send_rows`: entries may repeat.
All inputs are finite; a program needn't handle non-finite values.
Results may differ from a plain program's by a relative error of at most 0.0061.
Values may be sent and summed in bfloat16 or wider, within the bound.
No kernel may reach another device: no remote copies, remote signals or barrier semaphores. Data moves between devices by JAX's collectives and lax.ppermute only.
A program may use at most 64 MiB of HBM per device.

v0:
```python
import jax
import jax.numpy as jnp
from jax import lax
from jax.sharding import PartitionSpec as P


def passed_along(shard, axis, by):
    devices = lax.axis_size(axis)
    return lax.ppermute(shard, axis, [(i, (i + by) % devices) for i in range(devices)])


def slope(value):
    sig = jax.nn.sigmoid(value)
    return sig * (1.0 + value * (1.0 - sig))


def mean_rows(table, nbrs, count):
    total = jnp.zeros((nbrs.shape[0], table.shape[1]), jnp.float32)
    for slot in range(nbrs.shape[1]):
        picked = table[nbrs[:, slot]].astype(jnp.float32)
        total = total + jnp.where((slot < count)[:, None], picked, 0.0)
    return total / count[:, None].astype(jnp.float32)


def spread(grad, nbrs, count, size):
    slots = jnp.arange(nbrs.shape[1], dtype=jnp.int32)
    factor = jnp.where(
        slots[None, :] < count[:, None], 1.0 / count[:, None].astype(jnp.float32), 0.0
    )
    terms = (grad[:, None, :] * factor[:, :, None]).reshape(-1, grad.shape[1])
    return jax.ops.segment_sum(terms, nbrs.reshape(-1), num_segments=size)


def body(
    face_grid,
    first_nbrs,
    first_count,
    w_first,
    b_first,
    send_rows,
    second_nbrs,
    second_count,
    w_in,
    w_out,
    out_grad,
):
    targets = first_nbrs.shape[0]
    agg_first = (
        face_grid[:targets].astype(jnp.float32) + mean_rows(face_grid, first_nbrs, first_count)
    ).astype(jnp.bfloat16)
    partial_value = jnp.dot(agg_first, w_first, preferred_element_type=jnp.float32)
    pre_own = lax.psum_scatter(partial_value, "feat", scatter_dimension=0, tiled=True) + b_first
    hidden_own = jax.nn.silu(pre_own).astype(jnp.bfloat16)
    table = lax.all_gather(hidden_own, "feat", axis=0, tiled=True)
    received = passed_along(table[send_rows], "dp", 1)
    extended = jnp.concatenate([table, received], axis=0)
    agg_second = (
        hidden_own.astype(jnp.float32) + mean_rows(extended, second_nbrs, second_count)
    ).astype(jnp.bfloat16)
    pre_mlp = jnp.dot(agg_second, w_in, preferred_element_type=jnp.float32)
    act_mlp = jax.nn.silu(pre_mlp).astype(jnp.bfloat16)
    embed = (
        hidden_own.astype(jnp.float32) + jnp.dot(act_mlp, w_out, preferred_element_type=jnp.float32)
    ).astype(jnp.bfloat16)
    grad_act = lax.dot_general(
        out_grad, w_out, (((1,), (1,)), ((), ())), preferred_element_type=jnp.float32
    )
    grad_pre_mlp = (grad_act * slope(pre_mlp)).astype(jnp.bfloat16)
    grad_agg = lax.dot_general(
        grad_pre_mlp, w_in, (((1,), (1,)), ((), ())), preferred_element_type=jnp.float32
    )
    grad_ext = spread(grad_agg, second_nbrs, second_count, extended.shape[0])
    full_rows = table.shape[0]
    returned = passed_along(grad_ext[full_rows:].astype(jnp.bfloat16), "dp", -1).astype(jnp.float32)
    table_grad = grad_ext[:full_rows].at[send_rows].add(returned)
    own_terms = out_grad.astype(jnp.float32) + grad_agg
    grad_own = (
        lax.psum_scatter(
            table_grad.astype(jnp.bfloat16), "feat", scatter_dimension=0, tiled=True
        ).astype(jnp.float32)
        + own_terms
    )
    grad_pre_own = (grad_own * slope(pre_own)).astype(jnp.bfloat16)
    grad_pre_first = lax.all_gather(grad_pre_own, "feat", axis=0, tiled=True)
    slice_grad = lax.dot_general(
        agg_first, grad_pre_first, (((0,), (0,)), ((), ())), preferred_element_type=jnp.float32
    )
    grad_first = lax.psum(slice_grad, "dp")
    return (embed, grad_first)


def solution(mesh):
    return jax.shard_map(
        body,
        mesh=mesh,
        in_specs=(
            P("dp", "feat"),
            P("dp", None),
            P("dp"),
            P("feat", None),
            P(),
            P("dp"),
            P(("dp", "feat"), None),
            P(("dp", "feat")),
            P(),
            P(),
            P(("dp", "feat"), None),
        ),
        out_specs=(P(("dp", "feat"), None), P("feat", None)),
        check_vma=False,
    )
```

profile of v0, /device:TPU:8, one launch (start us, length us, event | category | flops | bytes accessed | tf_op | source)
XLA Modules:
  0.0 828.4 jit_solution(5859287706951482798)
XLA Ops:
  8.7 4.6 copy.22
  13.4 11.2 %gather_fusion = bf16[2048,320]{1,0:T(8,128)(2,1)} fusion(bf16[4096,320]{1,0:T(8,128)(2,1)} %copy.22, s32[2048]{0:T(1024)S(1)} %broadcast_clamp_fusion.7), kind=kCustom, calls=%fused_computation | custom fusion | bytes 2629632 | tf_op jit(solution)/shard_map/gather | solution.py:20
  24.6 11.2 %gather_fusion.1 = bf16[2048,320]{1,0:T(8,128)(2,1)} fusion(bf16[4096,320]{1,0:T(8,128)(2,1)} %copy.22, s32[2048]{0:T(1024)S(1)} %broadcast_clamp_fusion.6), kind=kCustom, calls=%fused_computation.1 | custom fusion | bytes 2629632 | tf_op jit(solution)/shard_map/gather | solution.py:20
  35.8 11.2 %gather_fusion.2 = bf16[2048,320]{1,0:T(8,128)(2,1)} fusion(bf16[4096,320]{1,0:T(8,128)(2,1)} %copy.22, s32[2048]{0:T(1024)S(1)} %broadcast_clamp_fusion.5), kind=kCustom, calls=%fused_computation.2 | custom fusion | bytes 2629632 | tf_op jit(solution)/shard_map/gather | solution.py:20
  47.0 11.2 %gather_fusion.3 = bf16[2048,320]{1,0:T(8,128)(2,1)} fusion(bf16[4096,320]{1,0:T(8,128)(2,1)} %copy.22, s32[2048]{0:T(1024)S(1)} %broadcast_clamp_fusion.4), kind=kCustom, calls=%fused_computation.3 | custom fusion | bytes 2629632 | tf_op jit(solution)/shard_map/gather | solution.py:20
  58.1 11.2 %gather_fusion.4 = bf16[2048,320]{1,0:T(8,128)(2,1)} fusion(bf16[4096,320]{1,0:T(8,128)(2,1)} %copy.22, s32[2048]{0:T(1024)S(1)} %broadcast_clamp_fusion.3), kind=kCustom, calls=%fused_computation.4 | custom fusion | bytes 2629632 | tf_op jit(solution)/shard_map/gather | solution.py:20
  69.3 11.2 %gather_fusion.5 = bf16[2048,320]{1,0:T(8,128)(2,1)} fusion(bf16[4096,320]{1,0:T(8,128)(2,1)} %copy.22, s32[2048]{0:T(1024)S(1)} %broadcast_clamp_fusion.2), kind=kCustom, calls=%fused_computation.5 | custom fusion | bytes 2629632 | tf_op jit(solution)/shard_map/gather | solution.py:20
  80.5 11.2 %gather_fusion.6 = bf16[2048,320]{1,0:T(8,128)(2,1)} fusion(bf16[4096,320]{1,0:T(8,128)(2,1)} %copy.22, s32[2048]{0:T(1024)S(1)} %broadcast_clamp_fusion.1), kind=kCustom, calls=%fused_computation.6 | custom fusion | bytes 2629632 | tf_op jit(solution)/shard_map/gather | solution.py:20
  91.7 11.2 %gather_fusion.7 = bf16[2048,320]{1,0:T(8,128)(2,1)} fusion(bf16[4096,320]{1,0:T(8,128)(2,1)} %copy.22, s32[2048]{0:T(1024)S(1)} %broadcast_clamp_fusion), kind=kCustom, calls=%fused_computation.7 | custom fusion | bytes 2629632 | tf_op jit(solution)/shard_map/gather | solution.py:20
  102.8 8.9 %add_convert_fusion = bf16[2048,320]{1,0:T(8,128)(2,1)S(1)} fusion(bf16[2048,320]{1,0:T(8,128)(2,1)} %gather_fusion.7, bf16[2048,320]{1,0:T(8,128)(2,1)} %gather_fusion.6, bf16[2048,320]{1,0:T(8,128)(2,1)} %gather_fusion.5, bf16[2048,320]{1,0:T(8,128)(2,1)} %gather_fusion.4, bf16[2048,320]{1,0:T(8,128)(2,1)} %gather_fusion.3, ...), kind=kLoop, calls=%fused_computation.19 | loop fusion | flops 17694720 | bytes 13131776 | tf_op jit(solution)/shard_map/convert_element_type | solution.py:50
  111.8 2.0 fusion.40
  113.9 220.8 %reduce-scatter.3.cloned.1.call-done = f32[64,256]{1,0:T(8,128)} async-done(((f32[2048,256]{1,0:T(8,128)}), f32[64,256]{1,0:T(8,128)}) %reduce-scatter.3.cloned.1.call-update) | async-done | bytes 65552 | tf_op jit(solution)/shard_map/reduce_scatter | solution.py:52
  336.6 75.6 %all-gather.3.cloned.1.call-done = bf16[2048,256]{1,0:T(8,128)(2,1)} async-done(((bf16[64,256]{1,0:T(8,128)(2,1)}), bf16[2048,256]{1,0:T(8,128)(2,1)}) %all-gather.3.cloned.1.call-update) | async-done | bytes 1048592 | tf_op jit(solution)/shard_map/all_gather | solution.py:54
  412.2 3.6 gather_fusion.8
  417.3 5.8 collective-permute-done
  423.8 2.1 gather_fusion.10
  426.0 2.2 gather_fusion.11
  428.2 2.1 gather_fusion.12
  430.3 2.1 gather_fusion.13
  432.5 2.1 gather_fusion.14
  434.6 2.1 gather_fusion.15
  436.8 2.1 gather_fusion.9
  438.9 2.1 gather_fusion.16
  441.9 5.1 scatter_custom_fusion
  448.1 3.1 slice.112
  451.9 6.0 scatter_custom_fusion.1
  457.9 2.7 convert_element_type.125
  460.7 215.0 %reduce-scatter.5.cloned.1.call-done = bf16[64,256]{1,0:T(8,128)(2,1)} async-done(((bf16[2048,256]{1,0:T(8,128)(2,1)}), bf16[64,256]{1,0:T(8,128)(2,1)}) %reduce-scatter.5.cloned.1.call-update) | async-done | bytes 32784 | tf_op jit(solution)/shard_map/reduce_scatter | solution.py:78
  677.2 75.9 %all-gather.5.cloned.1.call-done = bf16[2048,256]{1,0:T(8,128)(2,1)} async-done(((bf16[64,256]{1,0:T(8,128)(2,1)}), bf16[2048,256]{1,0:T(8,128)(2,1)}) %all-gather.5.cloned.1.call-update) | async-done | bytes 1048592 | tf_op jit(solution)/shard_map/all_gather | solution.py:84
  753.1 2.5 fusion.41
  756.6 63.6 %all-reduce.2.cloned.1.call-done = f32[320,256]{1,0:T(8,128)} async-done(((f32[320,256]{1,0:T(8,128)}), f32[320,256]{1,0:T(8,128)}) %all-reduce.2.cloned.1.call-update) | async-done | bytes 327696 | tf_op jit(solution)/shard_map/psum | solution.py:88
  820.1 1.7 copy.35
  (70 shorter events, 10.7 us)
Async XLA Ops:
  7.2 433.9 %copy-start = (bf16[256,1024]{1,0:T(8,128)(2,1)S(1)}, bf16[256,1024]{1,0:T(8,128)(2,1)}, u32[]{:S(2)}) copy-start(bf16[256,1024]{1,0:T(8,128)(2,1)} %param.19) | copy-start | bytes 1572868
  7.2 327.5 %reduce-scatter.3.cloned.1.call-start = ((), (), s32[]{:S(2)}) async-start(), calls=%async_computation.2 | async-start | bytes 2162688 | tf_op jit(solution)/shard_map/reduce_scatter | solution.py:52
  8.7 4.6 copy-start.5
  102.8 8.9 %copy-start.3 = (bf16[320,256]{1,0:T(8,128)(2,1)S(1)}, bf16[320,256]{1,0:T(8,128)(2,1)}, u32[]{:S(2)}) copy-start(bf16[320,256]{1,0:T(8,128)(2,1)} %param.14) | copy-start | bytes 491524
  113.8 220.9 %copy-start.8 = (f32[256]{0:T(256)S(1)}, f32[256]{0:T(256)}, u32[]{:S(2)}) copy-start(f32[256]{0:T(256)} %param.15) | copy-start | bytes 3076
  113.8 222.6 %copy-start.10 = (s32[512]{0:T(512)S(1)}, s32[512]{0:T(512)}, u32[]{:S(2)}) copy-start(s32[512]{0:T(512)} %param.16) | copy-start | bytes 6148
  113.8 222.7 %copy-start.7 = (s32[64,8]{0,1:T(8,128)S(1)}, s32[64,8]{0,1:T(8,128)}, u32[]{:S(2)}) copy-start(s32[64,8]{0,1:T(8,128)} %param.17) | copy-start | bytes 6148
  113.8 222.7 %copy-start.9 = (s32[64]{0:T(128)S(1)}, s32[64]{0:T(128)}, u32[]{:S(2)}) copy-start(s32[64]{0:T(128)} %param.18) | copy-start | bytes 772
  113.8 298.4 %all-gather.3.cloned.1.call-start = ((), (), s32[]{:S(2)}) async-start(), calls=%async_computation.3 | async-start | bytes 1081344 | tf_op jit(solution)/shard_map/all_gather | solution.py:54
  336.2 339.6 %reduce-scatter.5.cloned.1.call-start = ((), (), s32[]{:S(2)}) async-start(), calls=%async_computation.4 | async-start | bytes 1081344 | tf_op jit(solution)/shard_map/reduce_scatter | solution.py:78
  412.2 3.9 copy-start.1
  415.9 7.2 collective-permute-start
  417.3 23.8 %copy-start.4 = (bf16[64,256]{1,0:T(8,128)(2,1)S(1)}, bf16[64,256]{1,0:T(8,128)(2,1)}, u32[]{:S(2)}) copy-start(bf16[64,256]{1,0:T(8,128)(2,1)} %multiply_convert_fusion.3) | copy-start | bytes 98308
  426.0 15.4 %copy-start.6 = (bf16[64,256]{1,0:T(8,128)(2,1)S(1)}, bf16[64,256]{1,0:T(8,128)(2,1)}, u32[]{:S(2)}) copy-start(bf16[64,256]{1,0:T(8,128)(2,1)} %param.21) | copy-start | bytes 98308
  426.0 15.4 %copy-start.11 = (bf16[1024,256]{1,0:T(8,128)(2,1)S(1)}, bf16[1024,256]{1,0:T(8,128)(2,1)}, u32[]{:S(2)}) copy-start(bf16[1024,256]{1,0:T(8,128)(2,1)} %param.20) | copy-start | bytes 1572868
  448.0 3.9 collective-permute-start.1
  457.9 217.8 %copy-start.2 = (f32[64,256]{1,0:T(8,128)S(1)}, f32[64,256]{1,0:T(8,128)}, u32[]{:S(2)}) copy-start(f32[64,256]{1,0:T(8,128)} %reduce-scatter.3.cloned.1.call-done) | copy-start | bytes 196612
  460.7 292.5 %all-gather.5.cloned.1.call-start = ((), (), s32[]{:S(2)}) async-start(), calls=%async_computation.5 | async-start | bytes 1081344 | tf_op jit(solution)/shard_map/all_gather | solution.py:84
  677.2 142.9 %all-reduce.2.cloned.1.call-start = ((), (), s32[]{:S(2)}) async-start(), calls=%async_computation.6 | async-start | bytes 655360 | tf_op jit(solution)/shard_map/psum | solution.py:88
Sparse Core Ops, SparseCore 0:
  113.9 220.6 reduce-scatter.2
  337.8 74.3 all-gather.2
  460.8 214.9 reduce-scatter.4
  678.8 74.3 all-gather.4
  755.9 64.2 all-reduce.1
where the time goes:
time: 830 us; the launch traced here: 828 us
  waiting for transfers between devices  658 us (79%)
  local copies, waits for them, and re-layouts  123 us (15%)
  other arithmetic  27.3 us (3%)
  between operations  14 us (2%)
    reduce_scatter x1, waiting for transfers between devices, body(): lax.psum_scatter(partial_value, 'feat', scatter_dimension=0, tiled=True)  221 us
    reduce_scatter x1, waiting for transfers between devices, body(): lax.psum_scatter(table_grad.astype(jnp.bfloat16), 'feat', scatter_dimensi...  215 us
    gather x16, local copies, waits for them, and re-layouts, mean_rows(): picked = table[nbrs[:, slot]].astype(jnp.float32)  107 us
    all_gather x1, waiting for transfers between devices, body(): grad_pre_first = lax.all_gather(grad_pre_own, 'feat', axis=0, tiled=True)  75.9 us
    all_gather x1, waiting for transfers between devices, body(): table = lax.all_gather(hidden_own, 'feat', axis=0, tiled=True)  75.6 us
    psum x1, waiting for transfers between devices, body(): grad_first = lax.psum(slice_grad, 'dp')  63.6 us
  transfers between devices with their start and end apart: 7, of which 7 were waited for; matrix products, arithmetic and copies ran while one was open for 1% of the time, Pallas kernels for 0%

commit v1 on v0

--- a/solution.py
+++ b/solution.py
@@ -85,7 +85,7 @@
     slice_grad = lax.dot_general(
         agg_first, grad_pre_first, (((0,), (0,)), ((), ())), preferred_element_type=jnp.float32
     )
-    grad_first = lax.psum(slice_grad, "dp")
+    grad_first = jnp.sum(lax.all_gather(slice_grad, "dp"), 0)
     return (embed, grad_first)
 
 

time: 830 us -> 795 us (0.958)
  waiting for transfers between devices: 658 us -> 620 us
    psum x1 -> x0, waiting for transfers between devices: 63.6 us -> none  [body(): grad_first = lax.psum(slice_grad, 'dp')]
    all_gather x0 -> x1, waiting for transfers between devices: none -> 26.4 us  [body(): grad_first = jnp.sum(lax.all_gather(slice_grad, 'dp'), 0)]
where the time goes in v1:
time: 795 us; the launch traced here: 792 us
  waiting for transfers between devices  620 us (78%)
  local copies, waits for them, and re-layouts  121 us (15%)
  other arithmetic  29.9 us (4%)
  between operations  14 us (2%)
    reduce_scatter x1, waiting for transfers between devices, body(): lax.psum_scatter(partial_value, 'feat', scatter_dimension=0, tiled=True)  221 us
    reduce_scatter x1, waiting for transfers between devices, body(): lax.psum_scatter(table_grad.astype(jnp.bfloat16), 'feat', scatter_dimensi...  215 us
    gather x16, local copies, waits for them, and re-layouts, mean_rows(): picked = table[nbrs[:, slot]].astype(jnp.float32)  107 us
    all_gather x1, waiting for transfers between devices, body(): grad_pre_first = lax.all_gather(grad_pre_own, 'feat', axis=0, tiled=True)  75.9 us
    all_gather x1, waiting for transfers between devices, body(): table = lax.all_gather(hidden_own, 'feat', axis=0, tiled=True)  75.6 us
    all_gather x1, waiting for transfers between devices, body(): grad_first = jnp.sum(lax.all_gather(slice_grad, 'dp'), 0)  26.4 us
  transfers between devices with their start and end apart: 7, of which 7 were waited for; matrix products, arithmetic and copies ran while one was open for 1% of the time, Pallas kernels for 0%

profile of v1, /device:TPU:8, one launch (start us, length us, event | category | flops | bytes accessed | tf_op | source)
XLA Modules:
  0.0 792.2 jit_solution(18360806083179991006)
XLA Ops:
  8.7 4.6 copy.22
  13.4 11.2 %gather_fusion = bf16[2048,320]{1,0:T(8,128)(2,1)} fusion(bf16[4096,320]{1,0:T(8,128)(2,1)} %copy.22, s32[2048]{0:T(1024)S(1)} %broadcast_clamp_fusion.7), kind=kCustom, calls=%fused_computation | custom fusion | bytes 2629632 | tf_op jit(solution)/shard_map/gather | solution.py:20
  24.6 11.2 %gather_fusion.1 = bf16[2048,320]{1,0:T(8,128)(2,1)} fusion(bf16[4096,320]{1,0:T(8,128)(2,1)} %copy.22, s32[2048]{0:T(1024)S(1)} %broadcast_clamp_fusion.6), kind=kCustom, calls=%fused_computation.1 | custom fusion | bytes 2629632 | tf_op jit(solution)/shard_map/gather | solution.py:20
  35.8 11.2 %gather_fusion.2 = bf16[2048,320]{1,0:T(8,128)(2,1)} fusion(bf16[4096,320]{1,0:T(8,128)(2,1)} %copy.22, s32[2048]{0:T(1024)S(1)} %broadcast_clamp_fusion.5), kind=kCustom, calls=%fused_computation.2 | custom fusion | bytes 2629632 | tf_op jit(solution)/shard_map/gather | solution.py:20
  47.0 11.2 %gather_fusion.3 = bf16[2048,320]{1,0:T(8,128)(2,1)} fusion(bf16[4096,320]{1,0:T(8,128)(2,1)} %copy.22, s32[2048]{0:T(1024)S(1)} %broadcast_clamp_fusion.4), kind=kCustom, calls=%fused_computation.3 | custom fusion | bytes 2629632 | tf_op jit(solution)/shard_map/gather | solution.py:20
  58.1 11.2 %gather_fusion.4 = bf16[2048,320]{1,0:T(8,128)(2,1)} fusion(bf16[4096,320]{1,0:T(8,128)(2,1)} %copy.22, s32[2048]{0:T(1024)S(1)} %broadcast_clamp_fusion.3), kind=kCustom, calls=%fused_computation.4 | custom fusion | bytes 2629632 | tf_op jit(solution)/shard_map/gather | solution.py:20
  69.3 11.2 %gather_fusion.5 = bf16[2048,320]{1,0:T(8,128)(2,1)} fusion(bf16[4096,320]{1,0:T(8,128)(2,1)} %copy.22, s32[2048]{0:T(1024)S(1)} %broadcast_clamp_fusion.2), kind=kCustom, calls=%fused_computation.5 | custom fusion | bytes 2629632 | tf_op jit(solution)/shard_map/gather | solution.py:20
  80.5 11.2 %gather_fusion.6 = bf16[2048,320]{1,0:T(8,128)(2,1)} fusion(bf16[4096,320]{1,0:T(8,128)(2,1)} %copy.22, s32[2048]{0:T(1024)S(1)} %broadcast_clamp_fusion.1), kind=kCustom, calls=%fused_computation.6 | custom fusion | bytes 2629632 | tf_op jit(solution)/shard_map/gather | solution.py:20
  91.7 11.2 %gather_fusion.7 = bf16[2048,320]{1,0:T(8,128)(2,1)} fusion(bf16[4096,320]{1,0:T(8,128)(2,1)} %copy.22, s32[2048]{0:T(1024)S(1)} %broadcast_clamp_fusion), kind=kCustom, calls=%fused_computation.7 | custom fusion | bytes 2629632 | tf_op jit(solution)/shard_map/gather | solution.py:20
  102.8 8.9 %add_convert_fusion = bf16[2048,320]{1,0:T(8,128)(2,1)S(1)} fusion(bf16[2048,320]{1,0:T(8,128)(2,1)} %gather_fusion.7, bf16[2048,320]{1,0:T(8,128)(2,1)} %gather_fusion.6, bf16[2048,320]{1,0:T(8,128)(2,1)} %gather_fusion.5, bf16[2048,320]{1,0:T(8,128)(2,1)} %gather_fusion.4, bf16[2048,320]{1,0:T(8,128)(2,1)} %gather_fusion.3, ...), kind=kLoop, calls=%fused_computation.19 | loop fusion | flops 17694720 | bytes 13131776 | tf_op jit(solution)/shard_map/convert_element_type | solution.py:50
  111.8 2.0 fusion.40
  113.9 220.8 %reduce-scatter.3.cloned.1.call-done = f32[64,256]{1,0:T(8,128)} async-done(((f32[2048,256]{1,0:T(8,128)}), f32[64,256]{1,0:T(8,128)}) %reduce-scatter.3.cloned.1.call-update) | async-done | bytes 65552 | tf_op jit(solution)/shard_map/reduce_scatter | solution.py:52
  336.6 75.6 %all-gather.5.cloned.1.call-done = bf16[2048,256]{1,0:T(8,128)(2,1)} async-done(((bf16[64,256]{1,0:T(8,128)(2,1)}), bf16[2048,256]{1,0:T(8,128)(2,1)}) %all-gather.5.cloned.1.call-update) | async-done | bytes 1048592 | tf_op jit(solution)/shard_map/all_gather | solution.py:54
  412.2 3.6 gather_fusion.8
  417.3 5.8 collective-permute-done
  423.8 2.1 gather_fusion.10
  426.0 2.2 gather_fusion.11
  428.2 2.1 gather_fusion.12
  430.3 2.1 gather_fusion.13
  432.5 2.1 gather_fusion.14
  434.6 2.1 gather_fusion.15
  436.8 2.1 gather_fusion.9
  438.9 2.1 gather_fusion.16
  441.9 5.1 scatter_custom_fusion
  448.1 3.1 slice.112
  451.9 6.0 scatter_custom_fusion.1
  457.9 2.7 convert_element_type.125
  460.7 215.0 %reduce-scatter.5.cloned.1.call-done = bf16[64,256]{1,0:T(8,128)(2,1)} async-done(((bf16[2048,256]{1,0:T(8,128)(2,1)}), bf16[64,256]{1,0:T(8,128)(2,1)}) %reduce-scatter.5.cloned.1.call-update) | async-done | bytes 32784 | tf_op jit(solution)/shard_map/reduce_scatter | solution.py:78
  677.2 75.9 %all-gather.7.cloned.1.call-done = bf16[2048,256]{1,0:T(8,128)(2,1)} async-done(((bf16[64,256]{1,0:T(8,128)(2,1)}), bf16[2048,256]{1,0:T(8,128)(2,1)}) %all-gather.7.cloned.1.call-update) | async-done | bytes 1048592 | tf_op jit(solution)/shard_map/all_gather | solution.py:84
  753.1 2.5 fusion.41
  756.6 26.4 %all-gather.9.cloned.1.call-done = f32[2560,256]{1,0:T(8,128)} async-done(((f32[320,256]{1,0:T(8,128)}), f32[2560,256]{1,0:T(8,128)}) %all-gather.9.cloned.1.call-update) | async-done | bytes 2621456 | tf_op jit(solution)/shard_map/all_gather | solution.py:88
  783.0 2.7 reduce_sum.9
  (70 shorter events, 10.7 us)
Async XLA Ops:
  7.2 433.9 %copy-start = (bf16[256,1024]{1,0:T(8,128)(2,1)S(1)}, bf16[256,1024]{1,0:T(8,128)(2,1)}, u32[]{:S(2)}) copy-start(bf16[256,1024]{1,0:T(8,128)(2,1)} %param.19) | copy-start | bytes 1572868
  7.2 327.5 %reduce-scatter.3.cloned.1.call-start = ((), (), s32[]{:S(2)}) async-start(), calls=%async_computation.2 | async-start | bytes 2162688 | tf_op jit(solution)/shard_map/reduce_scatter | solution.py:52
  8.7 4.6 copy-start.5
  102.8 8.9 %copy-start.3 = (bf16[320,256]{1,0:T(8,128)(2,1)S(1)}, bf16[320,256]{1,0:T(8,128)(2,1)}, u32[]{:S(2)}) copy-start(bf16[320,256]{1,0:T(8,128)(2,1)} %param.14) | copy-start | bytes 491524
  113.8 220.9 %copy-start.8 = (f32[256]{0:T(256)S(1)}, f32[256]{0:T(256)}, u32[]{:S(2)}) copy-start(f32[256]{0:T(256)} %param.15) | copy-start | bytes 3076
  113.8 222.6 %copy-start.10 = (s32[512]{0:T(512)S(1)}, s32[512]{0:T(512)}, u32[]{:S(2)}) copy-start(s32[512]{0:T(512)} %param.16) | copy-start | bytes 6148
  113.8 222.7 %copy-start.7 = (s32[64,8]{0,1:T(8,128)S(1)}, s32[64,8]{0,1:T(8,128)}, u32[]{:S(2)}) copy-start(s32[64,8]{0,1:T(8,128)} %param.17) | copy-start | bytes 6148
  113.8 222.7 %copy-start.9 = (s32[64]{0:T(128)S(1)}, s32[64]{0:T(128)}, u32[]{:S(2)}) copy-start(s32[64]{0:T(128)} %param.18) | copy-start | bytes 772
  113.8 298.4 %all-gather.5.cloned.1.call-start = ((), (), s32[]{:S(2)}) async-start(), calls=%async_computation.3 | async-start | bytes 1081344 | tf_op jit(solution)/shard_map/all_gather | solution.py:54
  336.2 339.6 %reduce-scatter.5.cloned.1.call-start = ((), (), s32[]{:S(2)}) async-start(), calls=%async_computation.4 | async-start | bytes 1081344 | tf_op jit(solution)/shard_map/reduce_scatter | solution.py:78
  412.2 3.9 copy-start.1
  415.9 7.2 collective-permute-start
  417.3 23.8 %copy-start.4 = (bf16[64,256]{1,0:T(8,128)(2,1)S(1)}, bf16[64,256]{1,0:T(8,128)(2,1)}, u32[]{:S(2)}) copy-start(bf16[64,256]{1,0:T(8,128)(2,1)} %multiply_convert_fusion.3) | copy-start | bytes 98308
  426.0 15.4 %copy-start.6 = (bf16[64,256]{1,0:T(8,128)(2,1)S(1)}, bf16[64,256]{1,0:T(8,128)(2,1)}, u32[]{:S(2)}) copy-start(bf16[64,256]{1,0:T(8,128)(2,1)} %param.21) | copy-start | bytes 98308
  426.0 15.4 %copy-start.11 = (bf16[1024,256]{1,0:T(8,128)(2,1)S(1)}, bf16[1024,256]{1,0:T(8,128)(2,1)}, u32[]{:S(2)}) copy-start(bf16[1024,256]{1,0:T(8,128)(2,1)} %param.20) | copy-start | bytes 1572868
  448.0 3.9 collective-permute-start.1
  457.9 217.8 %copy-start.2 = (f32[64,256]{1,0:T(8,128)S(1)}, f32[64,256]{1,0:T(8,128)}, u32[]{:S(2)}) copy-start(f32[64,256]{1,0:T(8,128)} %reduce-scatter.3.cloned.1.call-done) | copy-start | bytes 196612
  460.7 292.5 %all-gather.7.cloned.1.call-start = ((), (), s32[]{:S(2)}) async-start(), calls=%async_computation.5 | async-start | bytes 1081344 | tf_op jit(solution)/shard_map/all_gather | solution.py:84
  677.2 105.8 %all-gather.9.cloned.1.call-start = ((), (), s32[]{:S(2)}) async-start(), calls=%async_computation.6 | async-start | bytes 2949120 | tf_op jit(solution)/shard_map/all_gather | solution.py:88
Sparse Core Ops, SparseCore 0:
  113.9 220.6 reduce-scatter.2
  337.8 74.3 all-gather.4
  460.8 214.9 reduce-scatter.4
  678.8 74.3 all-gather.6
  755.8 27.1 all-gather.8
